TPU v7x, 256 devices: a whole 4x4x8 slice. The times are simulated.
256 devices in a mesh: blk: 128 (over x_hi, z, y, core), grp: 2 (over x_lo).
Axes of the slice: x: 4 (x_hi: 2, x_lo: 2; x = x_hi * 2 + x_lo), y: 4, z: 8, core: 2. Of those that a mesh axis runs over, the one named last changes fastest.
Arguments:
- layer_one: bfloat16 [14336, 1024], P(('blk', 'grp')), may hold values from -6 to 6
- layer_two: bfloat16 [14336, 1024], P(('blk', 'grp')), may hold values from -6 to 6
- spread: int32 [2], replicated, may hold values from 1024 to 4096
Outputs:
- profiles: float32 [2, 14336], P(None, ('blk', 'grp'))
- alignment: float32 [], replicated
All inputs are finite; a program needn't handle non-finite values.
Results may differ from a plain program's by a relative error of at most 0.0003.
Values may be sent and summed in bfloat16 or wider, within the bound.
No kernel may reach another device: no remote copies, remote signals or barrier semaphores. Data moves between devices by JAX's collectives and lax.ppermute only.
A program may use at most 128 MiB of HBM per device.

v0:
```python
import functools
import jax
import jax.numpy as jnp
from jax import lax
from jax.sharding import Mesh
from jax.sharding import PartitionSpec as P

D = 1024
BLK = ("blk_0", "blk_1", "blk_2", "blk_3")
BLK_GRP = ("blk_0", "blk_1", "blk_2", "blk_3", "grp")


def by_axis(array, axes):
    return functools.reduce(lax.psum, axes, array)


def kernel_block(rows, sq_rows, cols, scale, offset):
    sq_cols = jnp.sum(cols.astype(jnp.float32) ** 2, axis=1)
    inner = lax.dot_general(
        rows, cols, (((1,), (1,)), ((), ())), preferred_element_type=jnp.float32
    )
    dist = sq_rows[:, None] + sq_cols[None, :] - 2.0 * inner
    return jnp.exp(-dist / (2.0 * scale)) - offset


def shards(layer_one, layer_two, spread):
    scales = spread.astype(jnp.float32)
    offsets = jnp.exp(-D / scales)
    stacked = jnp.stack([layer_one, layer_two])
    paired = lax.all_gather(stacked, "grp", axis=1, tiled=True)
    sq_pair = jnp.sum(paired.astype(jnp.float32) ** 2, axis=2)
    block = lax.all_gather(stacked, BLK, axis=1, tiled=True)
    first = kernel_block(paired[0], sq_pair[0], block[0], scales[0], offsets[0])
    second = kernel_block(paired[1], sq_pair[1], block[1], scales[1], offsets[1])
    first, second = (first, second)
    rows_acc = jnp.stack([jnp.sum(first, axis=1), jnp.sum(second, axis=1)])
    prods = jnp.stack([jnp.sum(first * second), jnp.sum(first * first), jnp.sum(second * second)])
    rows_acc, prods = (rows_acc, prods)
    own_rows = lax.psum_scatter(rows_acc, "grp", scatter_dimension=1, tiled=True)
    total = own_rows.shape[1] * lax.axis_size(BLK) * lax.axis_size("grp")
    row_terms = jnp.stack(
        [
            jnp.sum(own_rows[0]),
            jnp.sum(own_rows[1]),
            jnp.sum(own_rows[0] * own_rows[1]),
            jnp.sum(own_rows[0] * own_rows[0]),
            jnp.sum(own_rows[1] * own_rows[1]),
        ]
    )
    prods = by_axis(prods, BLK_GRP)
    row_terms = by_axis(row_terms, BLK_GRP)
    sum_one, sum_two = (row_terms[0], row_terms[1])
    c_cross, c_one, c_two = (row_terms[2], row_terms[3], row_terms[4])
    h_cross = prods[0] - 2.0 * c_cross / total + sum_one * sum_two / (total * total)
    h_one = prods[1] - 2.0 * c_one / total + sum_one * sum_one / (total * total)
    h_two = prods[2] - 2.0 * c_two / total + sum_two * sum_two / (total * total)
    alignment = h_cross / jnp.sqrt(h_one * h_two)
    profiles = jnp.stack(
        [own_rows[0] / jnp.sqrt(c_one / total), own_rows[1] / jnp.sqrt(c_two / total)]
    )
    return (profiles, alignment)


def solution(mesh):
    finer = Mesh(
        mesh.devices.reshape(2, 8, 4, 2, mesh.shape["grp"]),
        ("blk_0", "blk_1", "blk_2", "blk_3", "grp"),
    )
    return jax.shard_map(
        shards,
        mesh=finer,
        in_specs=(P(BLK_GRP, None), P(BLK_GRP, None), P()),
        out_specs=(P(None, BLK_GRP), P()),
        check_vma=False,
    )
```

profile of v0, /device:TPU:1, one launch (start us, length us, event | category | flops | bytes accessed | tf_op | source)
XLA Modules:
  0.0 312.2 jit_solution(16533642095395601667)
XLA Ops:
  7.2 1.7 pad_maximum_fusion
  8.9 0.7 convert_element_type.14
  9.6 0.6 fusion.16
  11.5 1.3 dynamic-slice
  13.4 0.7 divide_exponential_fusion
  14.0 0.6 fusion.17
  14.6 6.9 %all_gather.6 = bf16[2,112,1024]{2,1,0:T(8,128)(2,1)S(1)} all-gather(bf16[2,56,1024]{2,1,0:T(8,128)(2,1)} %pad_maximum_fusion), channel_id=1, replica_groups=mesh['blk_0'=2,'blk_1'=8,'blk_2'=4,'blk_3'=2,'grp'=2] {'grp'}, dimensions={1}, use_global_device_ids=true | all-gather | bytes 688128 | tf_op jit(solution)/shard_map/all_gather | solution.py:30
  21.5 0.2 multiply_reduce_fusion.5
  21.7 191.0 %all-gather.2.cloned.1.call-done = bf16[2,7168,1024]{2,1,0:T(8,128)(2,1)} async-done(((bf16[2,56,1024]{2,1,0:T(8,128)(2,1)}), bf16[2,7168,1024]{2,1,0:T(8,128)(2,1)}) %all-gather.2.cloned.1.call-update) | async-done | bytes 29360144 | tf_op jit(solution)/shard_map/all_gather | solution.py:32
  212.6 12.8 %multiply_reduce_fusion.1 = (f32[7168]{0:T(1024)S(1)}, f32[7168]{0:T(1024)S(1)}) fusion(bf16[2,7168,1024]{2,1,0:T(8,128)(2,1)} %all-gather.2.cloned.1.call-done), kind=kLoop, calls=%fused_computation.1 | loop fusion | flops 44025856 | bytes 29417472 | tf_op jit(solution)/shard_map/reduce_sum | solution.py:18
  225.4 9.0 %fusion.10 = f32[112,7168]{1,0:T(8,128)S(1)} fusion(bf16[2,7168,1024]{2,1,0:T(8,128)(2,1)} %all-gather.2.cloned.1.call-done, f32[]{:T(128)} %bitcast.12, f32[]{:T(128)} %bitcast.11, f32[7168]{0:T(1024)S(1)} %get-tuple-element.3, f32[112]{0:T(128)S(1)} %get-tuple-element.26, bf16[2,112,1024]{2,1,0:T(8,128)(2,1)S(1)} %all_gather.6), kind=kOutput, calls=%fused_computation.14 | convolution fusion | flops 1648984064 | bytes 18150912 | tf_op jit(solution)/shard_map/dot_general | solution.py:19
  234.5 10.3 %multiply_reduce_fusion.4 = (f32[]{:T(128)}, f32[]{:T(128)}, f32[112]{0:T(128)S(1)}, f32[]{:T(128)}, f32[112]{0:T(128)S(1)}) fusion(f32[112,7168]{1,0:T(8,128)S(1)} %fusion.10, f32[]{:T(128)} %bitcast.6, f32[]{:T(128)} %bitcast.5, bf16[2,7168,1024]{2,1,0:T(8,128)(2,1)} %all-gather.2.cloned.1.call-done, bf16[2,112,1024]{2,1,0:T(8,128)(2,1)S(1)} %all_gather.6, ...), kind=kOutput, calls=%fused_computation.20 | convolution fusion | flops 1655406336 | bytes 18151820 | tf_op jit(solution)/shard_map/dot_general | solution.py:19
  244.8 3.8 %all-reduce = f32[2,112]{1,0:T(2,128)S(1)} all-reduce(f32[2,112]{1,0:T(2,128)S(1)} %pad_maximum_fusion.1), channel_id=2, replica_groups=mesh['blk_0'=2,'blk_1'=8,'blk_2'=4,'blk_3'=2,'grp'=2] {'grp'}, use_global_device_ids=true, to_apply=%region_5.0.clone | all-reduce | flops 224 | bytes 1792
  248.5 0.1 constant_dynamic-slice_fusion
  248.6 0.7 multiply_reduce_fusion.6
  249.3 2.0 pad_maximum_fusion.3
  251.3 3.2 %stack.64 = f32[5]{0:T(128)S(1)} concatenate(f32[1]{0:T(128)} %bitcast.14, f32[1]{0:T(128)} %bitcast.15, f32[1]{0:T(128)} %bitcast.16, f32[1]{0:T(128)} %bitcast.17, f32[1]{0:T(128)} %bitcast.18), dimensions={0} | concatenate | bytes 40 | tf_op jit(solution)/shard_map/stack | solution.py:41
  254.5 5.3 %all-reduce.5 = (f32[5]{0:T(128)S(1)}, f32[3]{0:T(128)S(1)}) all-reduce(f32[5]{0:T(128)S(1)} %stack.64, f32[3]{0:T(128)S(1)} %pad_maximum_fusion.3), channel_id=1, replica_groups=mesh['blk_0'=2,'blk_1'=8,'blk_2'=4,'blk_3'=2,'grp'=2] {'blk_0'}, use_global_device_ids=true, to_apply=%region_11.0 | all-reduce | flops 8 | bytes 64 | tf_op jit(solution)/shard_map/psum | solution.py:14
  259.8 11.7 %all-reduce.1 = (f32[5]{0:T(128)S(1)}, f32[3]{0:T(128)S(1)}) all-reduce(f32[5]{0:T(128)S(1)} %get-tuple-element.22, f32[3]{0:T(128)S(1)} %get-tuple-element.23), channel_id=1, replica_groups=mesh['blk_0'=2,'blk_1'=8,'blk_2'=4,'blk_3'=2,'grp'=2] {'blk_1'}, use_global_device_ids=true, to_apply=%region_12.0 | all-reduce | flops 8 | bytes 64 | tf_op jit(solution)/shard_map/psum | solution.py:14
  271.5 8.4 %all-reduce.2 = (f32[5]{0:T(128)S(1)}, f32[3]{0:T(128)S(1)}) all-reduce(f32[5]{0:T(128)S(1)} %get-tuple-element.14, f32[3]{0:T(128)S(1)} %get-tuple-element.15), channel_id=1, replica_groups=mesh['blk_0'=2,'blk_1'=8,'blk_2'=4,'blk_3'=2,'grp'=2] {'blk_2'}, use_global_device_ids=true, to_apply=%region_13.0 | all-reduce | flops 8 | bytes 64 | tf_op jit(solution)/shard_map/psum | solution.py:14
  280.0 10.4 %all-reduce.4 = (f32[5]{0:T(128)S(1)}, f32[3]{0:T(128)S(1)}) all-reduce(f32[5]{0:T(128)S(1)} %get-tuple-element.16, f32[3]{0:T(128)S(1)} %get-tuple-element.17), channel_id=1, replica_groups=mesh['blk_0'=2,'blk_1'=8,'blk_2'=4,'blk_3'=2,'grp'=2] {'blk_3'}, use_global_device_ids=true, to_apply=%region_14.0 | all-reduce | flops 8 | bytes 64 | tf_op jit(solution)/shard_map/psum | solution.py:14
  290.4 3.8 %all-reduce.3 = (f32[5]{0:T(128)S(1)}, f32[3]{0:T(128)S(1)}) all-reduce(f32[5]{0:T(128)S(1)} %get-tuple-element.20, f32[3]{0:T(128)S(1)} %get-tuple-element.21), channel_id=1, replica_groups=mesh['blk_0'=2,'blk_1'=8,'blk_2'=4,'blk_3'=2,'grp'=2] {'grp'}, use_global_device_ids=true, to_apply=%region_15.0 | all-reduce | flops 8 | bytes 64 | tf_op jit(solution)/shard_map/psum | solution.py:14
  294.2 0.7 fusion.14
  303.7 0.6 pad_maximum_fusion.2
  (5 shorter events, 0.1 us)
Async XLA Ops:
  7.2 205.5 %all-gather.2.cloned.1.call-start = ((), (), s32[]{:S(2)}) async-start(), calls=%async_computation | async-start | bytes 29589504 | tf_op jit(solution)/shard_map/all_gather | solution.py:32
Sparse Core Ops, SparseCore 0:
  11.7 200.9 all-gather.1
where the time goes:
time: 313 us; the launch traced here: 312 us
  waiting for transfers between devices  191 us (61%)
  blocking collectives  50.3 us (16%)
  between operations  26 us (8%)
  matrix products  19.3 us (6%)
  other arithmetic  19.2 us (6%)
  local copies, waits for them, and re-layouts  6.45 us (2%)
    all_gather x1, waiting for transfers between devices, shards(): block = lax.all_gather(stacked, BLK, axis=1, tiled=True)  191 us
    psum x5, blocking collectives, by_axis(): return functools.reduce(lax.psum, axes, array)  39.7 us
    dot_general x2, matrix products, kernel_block(): lax.dot_general(rows, cols, (((1,), (1,)), ((), ())), preferred_element_t...  19.3 us
    reduce_sum x1, other arithmetic, kernel_block(): sq_cols = jnp.sum(cols.astype(jnp.float32) ** 2, axis=1)  12.8 us
    all_gather x1, blocking collectives, shards(): paired = lax.all_gather(stacked, 'grp', axis=1, tiled=True)  6.85 us
  transfers between devices with their start and end apart: 1, of which 1 were waited for; matrix products, arithmetic and copies ran while one was open for 1% of the time, Pallas kernels for 0%

commit v1 on v0

--- a/solution.py
+++ b/solution.py
@@ -29,7 +29,9 @@
     stacked = jnp.stack([layer_one, layer_two])
     paired = lax.all_gather(stacked, "grp", axis=1, tiled=True)
     sq_pair = jnp.sum(paired.astype(jnp.float32) ** 2, axis=2)
-    block = lax.all_gather(stacked, BLK, axis=1, tiled=True)
+    block = jnp.concatenate(
+        lax.all_to_all(jnp.stack([stacked] * lax.axis_size(BLK)), BLK, 0, 0), axis=1
+    )
     first = kernel_block(paired[0], sq_pair[0], block[0], scales[0], offsets[0])
     second = kernel_block(paired[1], sq_pair[1], block[1], scales[1], offsets[1])
     first, second = (first, second)

time: 313 us -> 815 us (2.60)
  waiting for transfers between devices: 191 us -> 568 us
  blocking collectives: 50.3 us -> 135 us
  local copies, waits for them, and re-layouts: 6.45 us -> 38.1 us
  starting transfers between devices: 0.04 us -> 16.9 us
  between operations: 26 us -> 12.7 us
    all_to_all x0 -> x1, waiting for transfers between devices: none -> 568 us  [shards(): lax.all_to_all(jnp.stack([stacked] * lax.axis_size(BLK)), BLK, 0, 0)]
    all_gather x1 -> x0, waiting for transfers between devices: 191 us -> none  [shards(): block = lax.all_gather(stacked, BLK, axis=1, tiled=True)]
    all_gather x1, blocking collectives: 6.85 us -> 70.9 us  [shards(): paired = lax.all_gather(stacked, 'grp', axis=1, tiled=True)]
    slice x0 -> x1, local copies, waits for them, and re-layouts: none -> 22.1 us  [shards(): block[1]]
    all_to_all x0 -> x1, starting transfers between devices: none -> 16.9 us  [shards(): lax.all_to_all(jnp.stack([stacked] * lax.axis_size(BLK)), BLK, 0, 0)]
    unnamed x1, blocking collectives: 3.77 us -> 15.6 us
    another operation x0 -> x1, local copies, waits for them, and re-layouts: none -> 10.1 us  [shards(): jnp.stack([stacked] * lax.axis_size(BLK))]
    psum x5, blocking collectives: 39.7 us -> 48.3 us  [by_axis(): return functools.reduce(lax.psum, axes, array)]
  transfers between devices with their start and end apart: 1 -> 1, of which waited for: 1 -> 1; matrix products, arithmetic and copies ran while one was open for 1% -> 0% of each run, Pallas kernels for 0% -> 0%
where the time goes in v1:
time: 815 us; the launch traced here: 814 us
  waiting for transfers between devices  568 us (70%)
  blocking collectives  135 us (17%)
  local copies, waits for them, and re-layouts  38.1 us (5%)
  matrix products  25.6 us (3%)
  other arithmetic  17.5 us (2%)
  starting transfers between devices  16.9 us (2%)
  between operations  12.7 us (2%)
    all_to_all x1, waiting for transfers between devices, shards(): lax.all_to_all(jnp.stack([stacked] * lax.axis_size(BLK)), BLK, 0, 0)  568 us
    all_gather x1, blocking collectives, shards(): paired = lax.all_gather(stacked, 'grp', axis=1, tiled=True)  70.9 us
    psum x5, blocking collectives, by_axis(): return functools.reduce(lax.psum, axes, array)  48.3 us
    dot_general x2, matrix products, kernel_block(): lax.dot_general(rows, cols, (((1,), (1,)), ((), ())), preferred_element_t...  25.6 us
    slice x1, local copies, waits for them, and re-layouts, shards(): block[1]  22.1 us
    all_to_all x1, starting transfers between devices, shards(): lax.all_to_all(jnp.stack([stacked] * lax.axis_size(BLK)), BLK, 0, 0)  16.9 us
  transfers between devices with their start and end apart: 1, of which 1 were waited for; matrix products, arithmetic and copies ran while one was open for 0% of the time, Pallas kernels for 0%

profile of v1, /device:TPU:1, one launch (start us, length us, event | category | flops | bytes accessed | tf_op | source)
XLA Modules:
  0.0 813.6 jit_solution(7591221915463627001)
XLA Ops:
  0.6 1.0 pad_maximum_fusion
  1.6 10.1 %stack.39 = bf16[128,2,56,1024]{3,2,1,0:T(8,128)(2,1)} broadcast(bf16[2,56,1024]{2,1,0:T(8,128)(2,1)S(1)} %pad_maximum_fusion), dimensions={1,2,3} | broadcast | bytes 29589504 | tf_op jit(solution)/shard_map/stack | solution.py:33
  11.7 16.9 %all-to-all-start = ((bf16[128,2,56,1024]{3,2,1,0:T(8,128)(2,1)}), bf16[128,2,56,1024]{3,2,1,0:T(8,128)(2,1)}, u32[]{:S(2)}, u32[]{:S(2)}) async-start(bf16[128,2,56,1024]{3,2,1,0:T(8,128)(2,1)} %stack.39), calls=%async_computation | async-start | bytes 58720256 | tf_op jit(solution)/shard_map/all_to_all | solution.py:33
  28.7 0.6 fusion.13
  30.6 0.6 dynamic-slice
  31.8 0.6 fusion.14
  32.4 70.9 %all_gather.3 = bf16[2,112,1024]{2,1,0:T(8,128)(2,1)S(1)} all-gather(bf16[2,56,1024]{2,1,0:T(8,128)(2,1)S(1)} %pad_maximum_fusion), channel_id=1, replica_groups=mesh['blk_0'=2,'blk_1'=8,'blk_2'=4,'blk_3'=2,'grp'=2] {'grp'}, dimensions={1}, use_global_device_ids=true | all-gather | bytes 688128 | tf_op jit(solution)/shard_map/all_gather | solution.py:30
  103.3 0.2 multiply_reduce_fusion.5
  103.5 567.9 %all-to-all-done = bf16[128,2,56,1024]{3,2,1,0:T(8,128)(2,1)} async-done(((bf16[128,2,56,1024]{3,2,1,0:T(8,128)(2,1)}), bf16[128,2,56,1024]{3,2,1,0:T(8,128)(2,1)}, u32[]{:S(2)}, u32[]{:S(2)}) %all-to-all-start) | async-done | bytes 29360160 | tf_op jit(solution)/shard_map/all_to_all | solution.py:33
  671.4 22.1 %fusion.10 = (bf16[1,128,56,1024]{3,2,0,1:T(8,128)(2,1)}, bf16[1,128,56,1024]{3,2,0,1:T(8,128)(2,1)}) fusion(bf16[2,128,56,1024]{3,2,0,1:T(8,128)(2,1)} %bitcast.3), kind=kLoop, calls=%fused_computation.35 | loop fusion | bytes 58720256 | tf_op jit(solution)/shard_map/slice | solution.py:36
  693.5 13.1 %multiply_reduce_fusion.1 = (f32[128,56]{1,0:T(8,128)S(1)}, f32[128,56]{1,0:T(8,128)S(1)}) fusion(bf16[2,128,56,1024]{3,2,0,1:T(8,128)(2,1)} %bitcast.3), kind=kLoop, calls=%fused_computation.1 | loop fusion | flops 44025856 | bytes 29417472 | tf_op jit(solution)/shard_map/reduce_sum | solution.py:18
  706.8 12.5 %fusion.6 = f32[112,7168]{1,0:T(8,128)} fusion(bf16[7168,1024]{1,0:T(8,128)(2,1)} %bitcast.40, f32[]{:T(128)} %bitcast.13, f32[]{:T(128)} %bitcast.12, f32[7168]{0:T(1024)S(1)} %add.77, f32[112]{0:T(128)S(1)} %get-tuple-element.28, bf16[2,112,1024]{2,1,0:T(8,128)(2,1)S(1)} %all_gather.3), kind=kOutput, calls=%fused_computation.10 | convolution fusion | flops 1648984064 | bytes 18149896 | tf_op jit(solution)/shard_map/dot_general | solution.py:19
  719.3 13.1 %multiply_reduce_fusion.4 = (f32[]{:T(128)}, f32[]{:T(128)}, f32[112]{0:T(128)S(1)}, f32[]{:T(128)}, f32[112]{0:T(128)S(1)}) fusion(f32[112,7168]{1,0:T(8,128)} %fusion.6, f32[]{:T(128)} %bitcast.7, f32[]{:T(128)} %bitcast.6, bf16[7168,1024]{1,0:T(8,128)(2,1)} %bitcast.39, bf16[2,112,1024]{2,1,0:T(8,128)(2,1)S(1)} %all_gather.3, f32[7168]{0:T(1024)S(1)} %add.72, ...), kind=kOutput, calls=%fused_computation.16 | convolution fusion | flops 1655406336 | bytes 18150804 | tf_op jit(solution)/shard_map/dot_general | solution.py:19
  732.4 15.6 %all-reduce = f32[2,112]{1,0:T(2,128)S(1)} all-reduce(f32[2,112]{1,0:T(2,128)S(1)} %pad_maximum_fusion.1), channel_id=2, replica_groups=mesh['blk_0'=2,'blk_1'=8,'blk_2'=4,'blk_3'=2,'grp'=2] {'grp'}, use_global_device_ids=true, to_apply=%region_5.0.clone | all-reduce | flops 224 | bytes 1792
  748.0 0.7 multiply_reduce_fusion.6
  748.7 2.0 pad_maximum_fusion.3
  750.7 3.2 stack.48
  754.0 5.3 all-reduce.5
  759.2 22.5 %all-reduce.1 = (f32[5]{0:T(128)S(1)}, f32[3]{0:T(128)S(1)}) all-reduce(f32[5]{0:T(128)S(1)} %get-tuple-element.22, f32[3]{0:T(128)S(1)} %get-tuple-element.23), channel_id=1, replica_groups=mesh['blk_0'=2,'blk_1'=8,'blk_2'=4,'blk_3'=2,'grp'=2] {'blk_1'}, use_global_device_ids=true, to_apply=%region_12.0 | all-reduce | flops 8 | bytes 64 | tf_op jit(solution)/shard_map/psum | solution.py:14
  781.7 6.1 all-reduce.2
  787.9 10.7 %all-reduce.4 = (f32[5]{0:T(128)S(1)}, f32[3]{0:T(128)S(1)}) all-reduce(f32[5]{0:T(128)S(1)} %get-tuple-element.16, f32[3]{0:T(128)S(1)} %get-tuple-element.17), channel_id=1, replica_groups=mesh['blk_0'=2,'blk_1'=8,'blk_2'=4,'blk_3'=2,'grp'=2] {'blk_3'}, use_global_device_ids=true, to_apply=%region_14.0 | all-reduce | flops 8 | bytes 64 | tf_op jit(solution)/shard_map/psum | solution.py:14
  798.5 3.8 all-reduce.3
  802.3 0.7 fusion.11
  811.2 0.6 pad_maximum_fusion.2
  (12 shorter events, 0.3 us)
Async XLA Ops:
  11.7 17.0 %copy-start = (s32[2]{0:T(128)S(1)}, s32[2]{0:T(128)}, u32[]{:S(2)}) copy-start(s32[2]{0:T(128)} %param.5) | copy-start | bytes 28
  11.7 18.9 %copy-start.1 = (u32[256]{0:T(256)S(1)}, u32[256]{0:T(256)}, u32[]{:S(2)}) copy-start(u32[256]{0:T(256)} %constant.38) | copy-start | bytes 3076
  11.7 659.7 %all-to-all-start = ((bf16[128,2,56,1024]{3,2,1,0:T(8,128)(2,1)}), bf16[128,2,56,1024]{3,2,1,0:T(8,128)(2,1)}, u32[]{:S(2)}, u32[]{:S(2)}) async-start(bf16[128,2,56,1024]{3,2,1,0:T(8,128)(2,1)} %stack.39), calls=%async_computation | async-start | bytes 58720256 | tf_op jit(solution)/shard_map/all_to_all | solution.py:33
